TPU v7x, 256 devices: a whole 4x4x8 slice. The times are simulated.
256 devices in a mesh: row: 8 (over y, core), col: 32 (over x, z).
Axes of the slice: x: 4, y: 4, z: 8, core: 2. Of those that a mesh axis runs over, the one named last changes fastest.
Arguments:
- tokens: bfloat16 [16384, 3072], P(('row', 'col')), may hold values from -6 to 6
- w_in: bfloat16 [3072, 12288], P('row', 'col'), may hold values from -0.109375 to 0.109375
- b_in: float32 [12288], P('col'), may hold values from -3 to 3
- conv_taps: float32 [27, 12288], P(None, 'col'), may hold values from -1.25 to 1.25
- conv_bias: float32 [12288], P('col'), may hold values from -3 to 3
- w_out: bfloat16 [12288, 3072], P('col', 'row'), may hold values from -0.0546875 to 0.0546875
- b_out: float32 [3072], replicated, may hold values from -3 to 3
Outputs:
- mixed: bfloat16 [16384, 3072], P(('row', 'col'))
All inputs are finite; a program needn't handle non-finite values.
Results may differ from a plain program's by a relative error of at most 0.0053.
Values may be sent and summed in bfloat16 or wider, within the bound.
A program may use at most 128 MiB of HBM per device.

v0:
```python
import jax
import jax.numpy as jnp
from jax import lax
from jax.sharding import PartitionSpec as P

HH = 32
WW = 32


def with_halo(shard, sides, width):
    for axis, dim in sides:
        count, length = (lax.axis_size(axis), shard.shape[dim])
        up = [(i, (i + 1) % count) for i in range(count - 1)]
        down = [(j, i) for i, j in up]
        last = lax.slice_in_dim(shard, length - width, length, axis=dim)
        initial = lax.slice_in_dim(shard, 0, width, axis=dim)
        before = lax.ppermute(last, axis, up)
        after = lax.ppermute(initial, axis, down)
        shard = jnp.concatenate([before, shard, after], axis=dim)
    return shard


def body(tokens, w_in, b_in, conv_taps, conv_bias, w_out, b_out):
    own_rows = tokens.shape[0]
    tok_rows = own_rows * lax.axis_size("col")
    hid_cols = w_in.shape[1]
    frame_count = tok_rows // (HH * WW)
    whole = lax.all_gather(tokens, "col", axis=0, tiled=True)
    before = jnp.dot(
        whole, lax.all_gather(w_in, "row", axis=0, tiled=True), preferred_element_type=jnp.float32
    )
    hidden = (before + b_in).astype(jnp.bfloat16).reshape(frame_count, HH, WW, hid_cols)
    extended = with_halo(hidden, (("row", 0),), 1)
    padded = jnp.pad(extended, ((0, 0), (1, 1), (1, 1), (0, 0)))
    summed = jnp.zeros((frame_count, HH, WW, hid_cols), jnp.float32)
    for offset in range(27):
        shift_t = offset // 9
        shift_h = offset // 3 % 3
        shift_w = offset % 3
        window = padded[
            shift_t : shift_t + frame_count, shift_h : shift_h + HH, shift_w : shift_w + WW, :
        ]
        summed = summed + window.astype(jnp.float32) * conv_taps[offset]
    activated = jax.nn.gelu(summed + conv_bias, approximate=True).astype(jnp.bfloat16)
    activated = activated.reshape(tok_rows, hid_cols)
    partial_value = jnp.dot(
        activated,
        lax.all_gather(w_out, "row", axis=1, tiled=True),
        preferred_element_type=jnp.float32,
    )
    shares = lax.psum_scatter(partial_value, "col", scatter_dimension=0, tiled=True)
    return (shares + b_out).astype(jnp.bfloat16)


def solution(mesh):
    placed = (
        P(("row", "col"), None),
        P("row", "col"),
        P("col"),
        P(None, "col"),
        P("col"),
        P("col", "row"),
        P(),
    )
    return jax.shard_map(
        body, mesh=mesh, in_specs=placed, out_specs=P(("row", "col"), None), check_vma=False
    )
```

profile of v0, /device:TPU:16, one launch (start us, length us, event | category | flops | bytes accessed | tf_op | source)
XLA Modules:
  0.0 494.6 jit_solution(7462746669944708098)
XLA Ops:
  6.5 0.7 all-gather.6.cloned.1.call-update
  7.3 0.0 all-gather.4.cloned.1.call-start
  7.3 0.7 all-gather.4.cloned.1.call-update
  8.0 0.0 all-gather.8.cloned.1.call-start
  8.1 31.4 %all-gather.6.cloned.1.call-done = bf16[3072,384]{1,0:T(8,128)(2,1)} async-done(((bf16[384,384]{1,0:T(8,128)(2,1)}), bf16[3072,384]{1,0:T(8,128)(2,1)}) %all-gather.6.cloned.1.call-update) | async-done | bytes 2359312 | tf_op jit(solution)/shard_map/all_gather | solution.py:30
  39.4 122.6 %all-gather.4.cloned.1.call-done = bf16[2048,3072]{1,0:T(8,128)(2,1)} async-done(((bf16[64,3072]{1,0:T(8,128)(2,1)}), bf16[2048,3072]{1,0:T(8,128)(2,1)}) %all-gather.4.cloned.1.call-update) | async-done | bytes 12582928 | tf_op jit(solution)/shard_map/all_gather | solution.py:28
  162.0 10.4 %add_convert_fusion = bf16[2048,384]{1,0:T(8,128)(2,1)S(1)} fusion(bf16[2048,3072]{1,0:T(8,128)(2,1)} %all-gather.4.cloned.1.call-done, bf16[3072,384]{1,0:T(8,128)(2,1)} %all-gather.6.cloned.1.call-done, f32[384]{0:T(512)} %param.9), kind=kOutput, calls=%fused_computation.21 | convolution fusion | flops 4833411072 | bytes 16516608 | tf_op jit(solution)/shard_map/dot_general | solution.py:29
  172.4 0.0 copy-start.2
  172.4 1.3 fusion.14
  173.7 1.9 collective-permute-start.1
  175.6 2.4 collective-permute-start
  178.1 0.0 all-gather.8.cloned.1.call-update
  178.1 0.0 reduce-scatter.2.cloned.1.call-start
  178.2 0.1 slice_reduce_fusion.26
  178.3 7.2 %collective-permute-done.1 = bf16[1,32,32,384]{3,2,1,0:T(8,128)(2,1)S(1)} collective-permute-done((bf16[1,32,32,384]{3,2,1,0:T(8,128)(2,1)}, bf16[1,32,32,384]{3,2,1,0:T(8,128)(2,1)S(1)}, u32[]{:S(2)}, u32[]{:S(2)}) %collective-permute-start.1) | collective-permute-done | bytes 786464 | tf_op jit(solution)/shard_map/ppermute | solution.py:18
  185.4 3.7 collective-permute-done
  189.2 1.9 select_maximum_fusion
  191.1 14.5 %fusion.13 = bf16[2,32,32,384]{3,2,1,0:T(8,128)(2,1)S(1)} fusion(bf16[2,32,32,384]{3,2,1,0:T(8,128)(2,1)S(1)} %bitcast.9, bf16[4,34,34,384]{3,2,1,0:T(8,128)(2,1)S(1)} %select_maximum_fusion, bf16[1,32,32,384]{3,2,1,0:T(8,128)(2,1)} %copy-done, bf16[1,32,32,384]{3,2,1,0:T(8,128)(2,1)} %copy-done.1, f32[384]{0:T(512)S(1)} %copy-done.4, ...), kind=kLoop, calls=%fused_computation.20 | loop fusion | flops 72351744 | bytes 42510336 | tf_op jit(solution)/shard_map/convert_element_type | solution.py:44
  205.6 0.0 all-gather.8.cloned.1.call-done
  205.6 13.3 %fusion.15 = f32[2048,3072]{1,0:T(8,128)} fusion(bf16[2048,384]{1,0:T(8,128)(2,1)S(1)} %bitcast.10, bf16[384,3072]{1,0:T(8,128)(2,1)} %all-gather.8.cloned.1.call-done), kind=kOutput, calls=%fused_computation.53 | convolution fusion | flops 4831838208 | bytes 29097984 | tf_op jit(solution)/shard_map/dot_general | solution.py:46
  219.0 0.0 reduce-scatter.2.cloned.1.call-update
  219.0 267.2 %reduce-scatter.2.cloned.1.call-done = f32[64,3072]{1,0:T(8,128)} async-done(((f32[2048,3072]{1,0:T(8,128)}), f32[64,3072]{1,0:T(8,128)}) %reduce-scatter.2.cloned.1.call-update) | async-done | bytes 786448 | tf_op jit(solution)/shard_map/reduce_scatter | solution.py:51
  486.2 0.0 copy-done.3
  486.2 1.9 add_convert_fusion.1
  (10 shorter events, 0.1 us)
Async XLA Ops:
  6.5 32.9 %all-gather.6.cloned.1.call-start = ((), (), s32[]{:S(2)}) async-start(), calls=%async_computation.2 | async-start | bytes 2654208 | tf_op jit(solution)/shard_map/all_gather | solution.py:30
  7.3 154.7 %all-gather.4.cloned.1.call-start = ((), (), s32[]{:S(2)}) async-start(), calls=%async_computation.1 | async-start | bytes 12976128 | tf_op jit(solution)/shard_map/all_gather | solution.py:28
  8.0 197.6 %all-gather.8.cloned.1.call-start = ((), (), s32[]{:S(2)}) async-start(), calls=%async_computation.3 | async-start | bytes 2654208 | tf_op jit(solution)/shard_map/all_gather | solution.py:48
  172.4 5.7 %copy-start.2 = (f32[27,384]{1,0:T(8,128)S(1)}, f32[27,384]{1,0:T(8,128)}, u32[]{:S(2)}) copy-start(f32[27,384]{1,0:T(8,128)} %param.10) | copy-start | bytes 124420
  173.7 11.7 %collective-permute-start.1 = (bf16[1,32,32,384]{3,2,1,0:T(8,128)(2,1)}, bf16[1,32,32,384]{3,2,1,0:T(8,128)(2,1)S(1)}, u32[]{:S(2)}, u32[]{:S(2)}) collective-permute-start(bf16[1,32,32,384]{3,2,1,0:T(8,128)(2,1)} %bitcast.2), channel_id=1, source_target_pairs={{32,0},{64,32},{96,64},{128,96},{160,128},{192,160},{224,192},{33,... | collective-permute-start | bytes 2359304 | tf_op jit(solution)/shard_map/ppermute | solution.py:18
  175.6 13.5 %collective-permute-start = (bf16[1,32,32,384]{3,2,1,0:T(8,128)(2,1)}, bf16[1,32,32,384]{3,2,1,0:T(8,128)(2,1)S(1)}, u32[]{:S(2)}, u32[]{:S(2)}) collective-permute-start(bf16[1,32,32,384]{3,2,1,0:T(8,128)(2,1)} %bitcast), channel_id=1, source_target_pairs={{0,32},{32,64},{64,96},{96,128},{128,160},{160,192},{192,224},{1,3... | collective-permute-start | bytes 2359304 | tf_op jit(solution)/shard_map/ppermute | solution.py:17
  178.1 308.1 %reduce-scatter.2.cloned.1.call-start = ((), (), s32[]{:S(2)}) async-start(), calls=%async_computation.4 | async-start | bytes 25952256 | tf_op jit(solution)/shard_map/reduce_scatter | solution.py:51
  185.4 5.6 %copy-start = (bf16[1,32,32,384]{3,2,1,0:T(8,128)(2,1)}, bf16[1,32,32,384]{3,2,1,0:T(8,128)(2,1)S(1)}, u32[]{:S(2)}) copy-start(bf16[1,32,32,384]{3,2,1,0:T(8,128)(2,1)S(1)} %collective-permute-done.1) | copy-start | bytes 2359300
  189.2 1.9 copy-start.1
  189.2 1.9 copy-start.4
  219.0 267.2 %copy-start.3 = (f32[3072]{0:T(1024)S(1)}, f32[3072]{0:T(1024)}, u32[]{:S(2)}) copy-start(f32[3072]{0:T(1024)} %param.13) | copy-start | bytes 36868
Sparse Core Ops, SparseCore 0:
  9.2 30.2 all-gather.5
  42.0 119.9 all-gather.3
  178.2 25.0 all-gather.7
  219.1 267.0 reduce-scatter.1
where the time goes:
time: 495 us
  waiting for transfers between devices  433 us (87%)
  matrix products  23.7 us (5%)
  other arithmetic  18.3 us (4%)
  between operations  13.2 us (3%)
    reduce_scatter x1, waiting for transfers between devices, body(): lax.psum_scatter(partial_value, 'col', scatter_dimension=0, tiled=True)  267 us
    all_gather x1, waiting for transfers between devices, body(): whole = lax.all_gather(tokens, 'col', axis=0, tiled=True)  123 us
    all_gather x1, waiting for transfers between devices, body(): lax.all_gather(w_in, 'row', axis=0, tiled=True)  31.4 us
    convert_element_type x1, other arithmetic, body(): jax.nn.gelu(summed + conv_bias, approximate=True).astype(jnp.bfloat16)  14.5 us
    dot_general x1, matrix products, body(): jnp.dot(activated, lax.all_gather(w_out, 'row', axis=1, tiled=True), pref...  13.3 us
    dot_general x1, matrix products, body(): jnp.dot(whole, lax.all_gather(w_in, 'row', axis=0, tiled=True), preferred...  10.4 us
  transfers between devices with their start and end apart: 6, of which 5 were waited for; matrix products, arithmetic and copies ran while one was open for 3% of the time, Pallas kernels for 0%

commit v1 on v0

--- a/solution.py
+++ b/solution.py
@@ -25,7 +25,12 @@
     tok_rows = own_rows * lax.axis_size("col")
     hid_cols = w_in.shape[1]
     frame_count = tok_rows // (HH * WW)
-    whole = lax.all_gather(tokens, "col", axis=0, tiled=True)
+    whole = jnp.concatenate(
+        lax.all_to_all(
+            jnp.stack(lax.axis_size("col") * [tokens]), split_axis=0, concat_axis=0, axis_name="col"
+        ),
+        0,
+    )
     before = jnp.dot(
         whole, lax.all_gather(w_in, "row", axis=0, tiled=True), preferred_element_type=jnp.float32
     )

time: 495 us -> 660 us (1.33)
  waiting for transfers between devices: 433 us -> 579 us
  starting transfers between devices: 4.43 us -> 17.2 us
  local copies, waits for them, and re-layouts: 1.48 us -> 8.58 us
    all_to_all x0 -> x1, waiting for transfers between devices: none -> 250 us  [body(): lax.all_to_all(jnp.stack(lax.axis_size('col') * [tokens]), split_axis=0,...]
    all_gather x1 -> x0, waiting for transfers between devices: 123 us -> none  [body(): whole = lax.all_gather(tokens, 'col', axis=0, tiled=True)]
    all_gather x1, waiting for transfers between devices: 0.02 us -> 18.3 us  [body(): lax.all_gather(w_out, 'row', axis=1, tiled=True)]
    all_to_all x0 -> x1, starting transfers between devices: none -> 11.6 us  [body(): lax.all_to_all(jnp.stack(lax.axis_size('col') * [tokens]), split_axis=0,...]
    another operation x0 -> x1, local copies, waits for them, and re-layouts: none -> 7.07 us  [body(): jnp.stack(lax.axis_size('col') * [tokens])]
  transfers between devices with their start and end apart: 6 -> 6, of which waited for: 5 -> 6; matrix products, arithmetic and copies ran while one was open for 3% -> 3% of each run, Pallas kernels for 0% -> 0%
where the time goes in v1:
time: 660 us
  waiting for transfers between devices  579 us (88%)
  matrix products  23.7 us (4%)
  other arithmetic  18.3 us (3%)
  starting transfers between devices  17.2 us (3%)
  between operations  13.2 us (2%)
  local copies, waits for them, and re-layouts  8.58 us (1%)
    reduce_scatter x1, waiting for transfers between devices, body(): lax.psum_scatter(partial_value, 'col', scatter_dimension=0, tiled=True)  270 us
    all_to_all x1, waiting for transfers between devices, body(): lax.all_to_all(jnp.stack(lax.axis_size('col') * [tokens]), split_axis=0,...  250 us
    all_gather x1, waiting for transfers between devices, body(): lax.all_gather(w_in, 'row', axis=0, tiled=True)  30.5 us
    all_gather x1, waiting for transfers between devices, body(): lax.all_gather(w_out, 'row', axis=1, tiled=True)  18.3 us
    convert_element_type x1, other arithmetic, body(): jax.nn.gelu(summed + conv_bias, approximate=True).astype(jnp.bfloat16)  14.5 us
    dot_general x1, matrix products, body(): jnp.dot(activated, lax.all_gather(w_out, 'row', axis=1, tiled=True), pref...  13.3 us
  transfers between devices with their start and end apart: 6, of which 6 were waited for; matrix products, arithmetic and copies ran while one was open for 3% of the time, Pallas kernels for 0%

profile of v1, /device:TPU:16, one launch (start us, length us, event | category | flops | bytes accessed | tf_op | source)
XLA Modules:
  0.0 660.0 jit_solution(1650704989009734922)
XLA Ops:
  6.5 7.1 %stack.2 = bf16[32,64,3072]{2,1,0:T(8,128)(2,1)} broadcast(bf16[64,3072]{1,0:T(8,128)(2,1)} %param.7), dimensions={1,2} | broadcast | bytes 12976128 | tf_op jit(solution)/shard_map/stack | solution.py:30
  13.6 11.6 %all-to-all-start = ((bf16[32,64,3072]{2,1,0:T(8,128)(2,1)}), bf16[32,64,3072]{2,1,0:T(8,128)(2,1)}, u32[]{:S(2)}, u32[]{:S(2)}) async-start(bf16[32,64,3072]{2,1,0:T(8,128)(2,1)} %stack.2), calls=%async_computation | async-start | bytes 25165824 | tf_op jit(solution)/shard_map/all_to_all | solution.py:29
  25.2 0.0 all-gather.3.cloned.1.call-start
  25.2 0.7 all-gather.3.cloned.1.call-update
  25.9 0.0 all-gather.5.cloned.1.call-start
  26.0 30.5 %all-gather.3.cloned.1.call-done = bf16[3072,384]{1,0:T(8,128)(2,1)} async-done(((bf16[384,384]{1,0:T(8,128)(2,1)}), bf16[3072,384]{1,0:T(8,128)(2,1)}) %all-gather.3.cloned.1.call-update) | async-done | bytes 2359312 | tf_op jit(solution)/shard_map/all_gather | solution.py:35
  56.5 249.7 %all-to-all-done = bf16[32,64,3072]{2,1,0:T(8,128)(2,1)} async-done(((bf16[32,64,3072]{2,1,0:T(8,128)(2,1)}), bf16[32,64,3072]{2,1,0:T(8,128)(2,1)}, u32[]{:S(2)}, u32[]{:S(2)}) %all-to-all-start) | async-done | bytes 12582944 | tf_op jit(solution)/shard_map/all_to_all | solution.py:29
  306.2 10.4 %add_convert_fusion = bf16[2048,384]{1,0:T(8,128)(2,1)S(1)} fusion(bf16[2048,3072]{1,0:T(8,128)(2,1)} %bitcast, bf16[3072,384]{1,0:T(8,128)(2,1)} %all-gather.3.cloned.1.call-done, f32[384]{0:T(512)S(1)} %copy-done.5), kind=kOutput, calls=%fused_computation.21 | convolution fusion | flops 4833411072 | bytes 16516608 | tf_op jit(solution)/shard_map/dot_general | solution.py:34
  316.6 0.0 copy-start.2
  316.6 1.3 fusion.14
  317.9 1.9 collective-permute-start
  319.8 3.6 collective-permute-start.1
  323.5 0.0 all-gather.5.cloned.1.call-update
  323.5 0.0 reduce-scatter.2.cloned.1.call-start
  323.6 0.1 slice_reduce_fusion.26
  323.7 7.7 %collective-permute-done = bf16[1,32,32,384]{3,2,1,0:T(8,128)(2,1)S(1)} collective-permute-done((bf16[1,32,32,384]{3,2,1,0:T(8,128)(2,1)}, bf16[1,32,32,384]{3,2,1,0:T(8,128)(2,1)S(1)}, u32[]{:S(2)}, u32[]{:S(2)}) %collective-permute-start) | collective-permute-done | bytes 786464 | tf_op jit(solution)/shard_map/ppermute | solution.py:17
  331.4 1.9 collective-permute-done.1
  333.3 1.9 select_maximum_fusion
  335.2 14.5 %fusion.13 = bf16[2,32,32,384]{3,2,1,0:T(8,128)(2,1)S(1)} fusion(bf16[2,32,32,384]{3,2,1,0:T(8,128)(2,1)S(1)} %bitcast.10, bf16[4,34,34,384]{3,2,1,0:T(8,128)(2,1)S(1)} %select_maximum_fusion, bf16[1,32,32,384]{3,2,1,0:T(8,128)(2,1)} %copy-done.1, bf16[1,32,32,384]{3,2,1,0:T(8,128)(2,1)} %copy-done, f32[384]{0:T(512)S(1)} %copy-done.4, ...), kind=kLoop, calls=%fused_computation.20 | loop fusion | flops 72351744 | bytes 42510336 | tf_op jit(solution)/shard_map/convert_element_type | solution.py:49
  349.7 18.3 %all-gather.5.cloned.1.call-done = bf16[384,3072]{1,0:T(8,128)(2,1)} async-done(((bf16[384,384]{1,0:T(8,128)(2,1)}), bf16[384,3072]{1,0:T(8,128)(2,1)}) %all-gather.5.cloned.1.call-update) | async-done | bytes 2359312 | tf_op jit(solution)/shard_map/all_gather | solution.py:53
  368.0 13.3 %fusion.15 = f32[2048,3072]{1,0:T(8,128)} fusion(bf16[2048,384]{1,0:T(8,128)(2,1)S(1)} %bitcast.11, bf16[384,3072]{1,0:T(8,128)(2,1)} %all-gather.5.cloned.1.call-done), kind=kOutput, calls=%fused_computation.53 | convolution fusion | flops 4831838208 | bytes 29097984 | tf_op jit(solution)/shard_map/dot_general | solution.py:51
  381.4 0.0 reduce-scatter.2.cloned.1.call-update
  381.4 270.2 %reduce-scatter.2.cloned.1.call-done = f32[64,3072]{1,0:T(8,128)} async-done(((f32[2048,3072]{1,0:T(8,128)}), f32[64,3072]{1,0:T(8,128)}) %reduce-scatter.2.cloned.1.call-update) | async-done | bytes 786448 | tf_op jit(solution)/shard_map/reduce_scatter | solution.py:56
  651.6 1.9 add_convert_fusion.1
  (12 shorter events, 0.1 us)
Async XLA Ops:
  13.6 292.6 %copy-start.5 = (f32[384]{0:T(512)S(1)}, f32[384]{0:T(512)}, u32[]{:S(2)}) copy-start(f32[384]{0:T(512)} %param.9) | copy-start | bytes 4612
  13.6 292.6 %all-to-all-start = ((bf16[32,64,3072]{2,1,0:T(8,128)(2,1)}), bf16[32,64,3072]{2,1,0:T(8,128)(2,1)}, u32[]{:S(2)}, u32[]{:S(2)}) async-start(bf16[32,64,3072]{2,1,0:T(8,128)(2,1)} %stack.2), calls=%async_computation | async-start | bytes 25165824 | tf_op jit(solution)/shard_map/all_to_all | solution.py:29
  25.2 31.3 %all-gather.3.cloned.1.call-start = ((), (), s32[]{:S(2)}) async-start(), calls=%async_computation.2 | async-start | bytes 2654208 | tf_op jit(solution)/shard_map/all_gather | solution.py:35
  25.9 342.1 %all-gather.5.cloned.1.call-start = ((), (), s32[]{:S(2)}) async-start(), calls=%async_computation.3 | async-start | bytes 2654208 | tf_op jit(solution)/shard_map/all_gather | solution.py:53
  316.6 7.0 %copy-start.2 = (f32[27,384]{1,0:T(8,128)S(1)}, f32[27,384]{1,0:T(8,128)}, u32[]{:S(2)}) copy-start(f32[27,384]{1,0:T(8,128)} %param.10) | copy-start | bytes 124420
  317.9 13.5 %collective-permute-start = (bf16[1,32,32,384]{3,2,1,0:T(8,128)(2,1)}, bf16[1,32,32,384]{3,2,1,0:T(8,128)(2,1)S(1)}, u32[]{:S(2)}, u32[]{:S(2)}) collective-permute-start(bf16[1,32,32,384]{3,2,1,0:T(8,128)(2,1)} %bitcast.1), channel_id=1, source_target_pairs={{0,32},{32,64},{64,96},{96,128},{128,160},{160,192},{192,224},{1,3... | collective-permute-start | bytes 2359304 | tf_op jit(solution)/shard_map/ppermute | solution.py:17
  319.8 13.5 %collective-permute-start.1 = (bf16[1,32,32,384]{3,2,1,0:T(8,128)(2,1)}, bf16[1,32,32,384]{3,2,1,0:T(8,128)(2,1)S(1)}, u32[]{:S(2)}, u32[]{:S(2)}) collective-permute-start(bf16[1,32,32,384]{3,2,1,0:T(8,128)(2,1)} %bitcast.3), channel_id=1, source_target_pairs={{32,0},{64,32},{96,64},{128,96},{160,128},{192,160},{224,192},{33,... | collective-permute-start | bytes 2359304 | tf_op jit(solution)/shard_map/ppermute | solution.py:18
  323.5 328.1 %reduce-scatter.2.cloned.1.call-start = ((), (), s32[]{:S(2)}) async-start(), calls=%async_computation.4 | async-start | bytes 25952256 | tf_op jit(solution)/shard_map/reduce_scatter | solution.py:56
  331.4 3.8 copy-start
  333.3 1.9 copy-start.1
  333.3 1.9 copy-start.4
  381.3 270.2 %copy-start.3 = (f32[3072]{0:T(1024)S(1)}, f32[3072]{0:T(1024)}, u32[]{:S(2)}) copy-start(f32[3072]{0:T(1024)} %param.13) | copy-start | bytes 36868
Sparse Core Ops, SparseCore 0:
  27.8 28.6 all-gather.2
  323.6 44.3 all-gather.4
  381.5 270.0 reduce-scatter.1
